TPU v7x, 32 devices: a whole 2x2x4 slice. The times are simulated.
32 devices in a mesh: gx: 2 (over y), gy: 4 (over x, core), gz: 4 (over z).
Axes of the slice: x: 2, y: 2, z: 4, core: 2. Of those that a mesh axis runs over, the one named last changes fastest.
Arguments:
- snapshots: bfloat16 [16, 64, 64, 256], P('gx', 'gy', 'gz'), may hold values from -1500 to 1500
- sketch: float32 [256, 256], replicated, may hold values from -0.5 to 1.5
- velocity: float32 [3, 16, 64, 64], P(None, 'gx', 'gy', 'gz'), may hold values from -4 to 4
- viscosity: float32 [16, 64, 64], P('gx', 'gy', 'gz'), may hold values from 0.2 to 2
Outputs:
- applied_modes: bfloat16 [16, 64, 64, 256], P('gx', 'gy', 'gz')
- reduced: float32 [256, 256], replicated
All inputs are finite; a program needn't handle non-finite values.
Results may differ from a plain program's by a relative error of at most 0.0015.
The roundings to bfloat16 on the way count: a program that leaves them out, or rounds other values in their place, can miss the bound.
Values may be sent and summed in bfloat16 or wider, within the bound.
No kernel may reach another device: no remote copies, remote signals or barrier semaphores. Data moves between devices by JAX's collectives and lax.ppermute only.
A program may use at most 64 MiB of HBM per device.

v0:
```python
import functools

import jax
import jax.numpy as jnp
from jax import lax
from jax.experimental import pallas as pl
from jax.experimental.pallas import tpu as pltpu
from jax.sharding import PartitionSpec as P

f32 = jnp.float32
bf16 = jnp.bfloat16
VMEM = pl.BlockSpec(memory_space=pltpu.VMEM)
SMEM = pl.BlockSpec(memory_space=pltpu.SMEM)
HBM = pl.BlockSpec(memory_space=pltpu.HBM)
PARAMS = pltpu.CompilerParams(vmem_limit_bytes=16 << 20)
TILE = 8
PANEL = 64


def split2(x):
    high = x.astype(bf16)
    return high, (x - high.astype(f32)).astype(bf16)


def split3(x):
    high = x.astype(bf16)
    return (high, *split2(x - high.astype(f32)))


def matmul(a, b, dim_a, dim_b):
    return lax.dot_general(a, b, (((dim_a,), (dim_b,)), ((), ())), preferred_element_type=f32)


def dot_f32(a, b, dim_a, dim_b):
    ah, am, al = split3(a)
    bh, bm, bl = split3(b)
    left = jnp.concatenate([ah, ah, am, am, ah, al], axis=dim_a)
    right = jnp.concatenate([bh, bm, bh, bm, bl, bh], axis=dim_b)
    return matmul(left, right, dim_a, dim_b)


def on_chip(shape, dtype):
    return pltpu.VMEM(shape, dtype)


def in_hbm(*values):
    return [pltpu.with_memory_space_constraint(value, pltpu.HBM) for value in values]


def held(*values):
    return [pltpu.with_memory_space_constraint(value, pltpu.VMEM) for value in values]


def sketch_kernel(
    scale,
    steps,
    flag_ref,
    snap_ref,
    sketch_ref,
    velocity_ref,
    viscosity_ref,
    out_ref,
    x1_ref,
    x2_ref,
    y1_ref,
    y2_ref,
    z1_ref,
    z2_ref,
    sent_ref,
    kept_ref,
    coef_ref,
    rows_ref,
    table_ref,
    parts_ref,
    gram_ref,
    flow_ref,
    sems,
):
    cells_x, cells_y, cells_z, columns = out_ref.shape
    half = columns // 2
    planes = cells_x // steps
    table = pltpu.make_async_copy(sketch_ref, table_ref, sems.at[steps])
    table.start()
    copies = []
    for i in range(steps):
        span = pl.ds(i * planes, planes)
        copies.append(pltpu.make_async_copy(snap_ref.at[span], rows_ref.at[span], sems.at[i]))
        copies[-1].start()
    flow = pltpu.make_async_copy(velocity_ref, flow_ref.at[:3], sems.at[steps + 1])
    flow.start()
    spread = pltpu.make_async_copy(viscosity_ref, flow_ref.at[3], sems.at[steps + 2])
    spread.start()
    table.wait()
    for i, part in enumerate(split3(table_ref[...])):
        parts_ref[i * columns : (i + 1) * columns, :] = part
    even = [flag_ref[k] == 0 for k in range(3)]
    for i in range(steps):
        copies[i].wait()
        span = slice(i * planes, (i + 1) * planes)
        rows = rows_ref[span].reshape(-1, columns)
        made = matmul(jnp.concatenate([rows, rows, rows], axis=1), parts_ref[...], 1, 0)
        made = made.astype(bf16)
        gram = matmul(made, made, 0, 0)
        for at, value in (
            (0, gram[:half, :half]),
            (half, gram[:half, half:]),
            (columns, gram[half:, half:]),
        ):
            value = value if i == 0 else gram_ref[at : at + half, :] + value
            gram_ref[at : at + half, :] = value * scale if i == steps - 1 else value
        out_ref[span] = made.reshape(planes, cells_y, cells_z, columns)
        field = out_ref[span]
        low_y, high_y = field[:, 0], field[:, cells_y - 1]
        y1_ref[span] = jnp.where(even[1], high_y, low_y)
        y2_ref[span] = jnp.where(even[1], low_y, high_y)
        low_z = field[:, :, 0, :].astype(f32)
        high_z = field[:, :, cells_z - 1, :].astype(f32)
        z1_ref[span] = jnp.where(even[2], high_z, low_z).astype(bf16)
        z2_ref[span] = jnp.where(even[2], low_z, high_z).astype(bf16)
    flow.wait()
    spread.wait()
    for k in range(4):
        for x in range(cells_x):
            plane = flow_ref[k, x].T
            coef_ref[k, x] = 0.5 * plane if k < 3 else plane
    low_x, high_x = out_ref[0], out_ref[cells_x - 1]
    x1_ref[...] = jnp.where(even[0], high_x, low_x)
    x2_ref[...] = jnp.where(even[0], low_x, high_x)
    size = sent_ref.shape[0]
    mine = pl.multiple_of(flag_ref[3] * size, size)
    other = pl.multiple_of((1 - flag_ref[3]) * size, size)
    kept_ref[...] = gram_ref[pl.ds(mine, size), :]
    sent_ref[...] = gram_ref[pl.ds(other, size), :]


def sketch_call(flags, snapshots, sketch, velocity, viscosity, scale):
    cells_x, cells_y, cells_z, columns = snapshots.shape
    half = columns // 2
    steps = 2
    return pl.pallas_call(
        functools.partial(sketch_kernel, scale, steps),
        in_specs=[SMEM] + [HBM] * 4,
        out_specs=[VMEM] * 10,
        out_shape=[
            on_chip(snapshots.shape, bf16),
            on_chip((cells_y, cells_z, columns), bf16),
            on_chip((cells_y, cells_z, columns), bf16),
            on_chip((cells_x, cells_z, columns), bf16),
            on_chip((cells_x, cells_z, columns), bf16),
            on_chip((cells_x, cells_y, columns), bf16),
            on_chip((cells_x, cells_y, columns), bf16),
            on_chip((3 * half // 2, half), f32),
            on_chip((3 * half // 2, half), f32),
            on_chip((4, cells_x, cells_z, cells_y), f32),
        ],
        scratch_shapes=[
            pltpu.VMEM(snapshots.shape, bf16),
            pltpu.VMEM(sketch.shape, f32),
            pltpu.VMEM((3 * columns, columns), bf16),
            pltpu.VMEM((3 * half, half), f32),
            pltpu.VMEM((4, cells_x, cells_y, cells_z), f32),
            pltpu.SemaphoreType.DMA((steps + 3,)),
        ],
        compiler_params=PARAMS,
        name="sketch",
    )(flags, *in_hbm(snapshots, sketch, velocity, viscosity))


def operator_kernel(
    scale,
    planes,
    flag_ref,
    s_ref,
    x1_ref,
    x2_ref,
    y1_ref,
    y2_ref,
    z1_ref,
    z2_ref,
    coef_ref,
    *refs,
):
    cells_x, cells_y, cells_z, columns = s_ref.shape
    first = planes[0]
    even = [flag_ref[k] == 0 for k in range(3)]
    if first == 0:
        image_ref, total_ref = refs
    else:
        sum_ref, image_ref, sent_ref, kept_ref, total_ref = refs
    for x in planes:
        for y in range(cells_y):
            middle = s_ref[x, y].astype(f32)
            if x > 0:
                before = s_ref[x - 1, y]
            else:
                before = jnp.where(even[0], x2_ref[y], x1_ref[y])
            if x < cells_x - 1:
                after = s_ref[x + 1, y]
            else:
                after = jnp.where(even[0], x1_ref[y], x2_ref[y])
            before, after = before.astype(f32), after.astype(f32)
            if y > 0:
                south = s_ref[x, y - 1]
            else:
                south = jnp.where(even[1], y2_ref[x], y1_ref[x])
            if y < cells_y - 1:
                north = s_ref[x, y + 1]
            else:
                north = jnp.where(even[1], y1_ref[x], y2_ref[x])
            south, north = south.astype(f32), north.astype(f32)
            z1, z2 = z1_ref[x, y : y + 1].astype(f32), z2_ref[x, y : y + 1].astype(f32)
            below, above = jnp.where(even[2], z2, z1), jnp.where(even[2], z1, z2)
            lower = jnp.concatenate([below, middle[:-1]], axis=0)
            upper = jnp.concatenate([middle[1:], above], axis=0)
            around = (after + before) + (north + south) + (upper + lower)

            def spread(k):
                return jnp.broadcast_to(coef_ref[k, x, :, y : y + 1], middle.shape)

            image = spread(3) * (6.0 * middle - around)
            image = image + spread(0) * (after - before)
            image = image + spread(1) * (north - south)
            image = image + spread(2) * (upper - lower)
            high, low = split2(image)
            at = ((x - first) * cells_y + y) * cells_z
            image_ref[at : at + cells_z, :columns] = high
            image_ref[at : at + cells_z, columns:] = low
        plane = s_ref[x]
        at = (x - first) * cells_y * cells_z
        high = image_ref[at : at + cells_y * cells_z, :columns]
        low = image_ref[at : at + cells_y * cells_z, columns:]
        base = plane.reshape(-1, columns)
        part = matmul(
            jnp.concatenate([base, base], axis=0), jnp.concatenate([high, low], axis=0), 0, 0
        )
        if x > first:
            part = total_ref[...] + part
        elif first > 0:
            part = sum_ref[...] + part
        if x < cells_x - 1:
            total_ref[...] = part
        else:
            total_ref[...] = part * scale
            size = columns // 2
            mine = pl.multiple_of(flag_ref[3] * size, size)
            other = pl.multiple_of((1 - flag_ref[3]) * size, size)
            for at in (0, size):
                kept_ref[at : at + size, :] = total_ref[pl.ds(mine, size), at : at + size]
                sent_ref[at : at + size, :] = total_ref[pl.ds(other, size), at : at + size]


def operator_calls(flags, sketched, halos, coefs, scale):
    cells_x, cells_y, cells_z, columns = sketched.shape
    half = cells_x // 2
    image = on_chip((half * cells_y * cells_z, 2 * columns), bf16)
    image0, partial = pl.pallas_call(
        functools.partial(operator_kernel, scale, range(half)),
        in_specs=[SMEM] + [VMEM] * 8,
        out_specs=[VMEM] * 2,
        out_shape=[image, on_chip((columns, columns), f32)],
        compiler_params=PARAMS,
        name="operator0",
    )(flags, *held(sketched, *halos, coefs))
    image1, sent, kept = pl.pallas_call(
        functools.partial(operator_kernel, scale, range(half, cells_x)),
        in_specs=[SMEM] + [VMEM] * 9,
        out_specs=[VMEM] * 3,
        out_shape=[image] + [on_chip((columns, columns // 2), f32)] * 2,
        scratch_shapes=[pltpu.VMEM((columns, columns), f32)],
        compiler_params=PARAMS,
        name="operator1",
    )(flags, *held(sketched, *halos, coefs, partial))
    return image0, image1, sent, kept


def total(values):
    values = list(values)
    while len(values) > 1:
        pairs = zip(values[::2], values[1::2])
        values = [a + b for a, b in pairs] + values[len(values) // 2 * 2 :]
    return values[0]


def eliminate(block, cells_ref):
    size = block.shape[0]
    sub = lax.broadcasted_iota(jnp.int32, (TILE, size), 0)
    lane = lax.broadcasted_iota(jnp.int32, (TILE, size), 1)
    tiles = [block[i : i + TILE, :] for i in range(0, size, TILE)]
    count = size // TILE
    pivots = []

    def full(value):
        return jnp.broadcast_to(value, (TILE, size))

    for s in range(count):
        at = s * TILE
        tile = tiles[s]
        cols = [
            [full(tiles[t][:, at + k : at + k + 1]) for k in range(TILE)] for t in range(s, count)
        ]
        for k in range(TILE):
            cells_ref[k * TILE : (k + 1) * TILE, :] = cols[0][k]
        a = [
            [cells_ref[pl.ds(k * TILE + i, TILE, stride=0), :] for k in range(i + 1)]
            for i in range(TILE)
        ]
        w = [[None] * TILE for _ in range(TILE)]
        r = []
        for j in range(TILE):
            r.append(1.0 / a[j][j])
            m = [a[i][j] * r[j] if i > j else None for i in range(TILE)]
            for i in range(j + 1, TILE):
                for k in range(j + 1, i + 1):
                    a[i][k] = a[i][k] - m[i] * a[k][j]
                for k in range(j):
                    w[i][k] = w[i][k] - m[i] * w[j][k]
                w[i][j] = -m[i]
        unit = []
        for k in range(TILE):
            col = jnp.where(sub == k, 1.0, 0.0)
            for i in range(k + 1, TILE):
                col = jnp.where(sub == i, w[i][k], col)
            unit.append(col)
        pivot = r[0]
        for i in range(1, TILE):
            pivot = jnp.where(sub == i, r[i], pivot)
        pivots.append(pivot[:, :1])
        new = total(unit[k] * full(tile[k : k + 1, :]) for k in range(TILE))
        for k in range(TILE):
            new = jnp.where(lane == at + k, unit[k], new)
        tiles[s] = new
        if s == count - 1:
            break
        rows = [full(new[k : k + 1, :]) * r[k] for k in range(TILE)]
        inside = (lane >= at) & (lane < at + TILE)
        for t in range(s + 1, count):
            col = cols[t - s]
            terms = []
            for k in range(TILE):
                factor = total([col[k]] + [w[k][i] * col[i] for i in range(k)])
                terms.append(factor * rows[k])
            tiles[t] = jnp.where(inside, 0.0, tiles[t]) - total(terms)
    result = jnp.concatenate(tiles, axis=0)
    row_b = lax.broadcasted_iota(jnp.int32, (size, size), 0)
    lane_b = lax.broadcasted_iota(jnp.int32, (size, size), 1)
    return jnp.where(lane_b <= row_b, result, 0.0), jnp.concatenate(pivots, axis=0)


def factor_kernel(start, *refs):
    refs, cells_ref = refs[:-1], refs[-1]
    if start == 0:
        flag_ref, part_ref, other_ref, out_ref, next_ref, state_ref = refs
        half = state_ref.shape[1] // 2
        own_first = flag_ref[3] == 0
        part, other = part_ref[...], other_ref[...]
        upper = jnp.where(own_first, part, other)
        under = jnp.where(own_first, other, part)
        both = jnp.concatenate([upper, under], axis=0)
        state_ref[:half, :half] = both[:half]
        state_ref[:half, half:] = both[half : 2 * half]
        state_ref[half:, :half] = jnp.zeros((half, half), f32)
        state_ref[half:, half:] = both[2 * half :]
    elif len(refs) == 3:
        state_ref, out_ref, next_ref = refs
    else:
        state_ref, out_ref = refs
        next_ref = None
    n = state_ref.shape[1]
    end = start + PANEL
    lane = lax.broadcasted_iota(jnp.int32, (PANEL, n), 1)
    unit, pivots = eliminate(state_ref[:PANEL, start:end], cells_ref)
    panel = dot_f32(unit, state_ref[:PANEL, :], 1, 0)
    pieces = [unit]
    if start:
        pieces = [jnp.zeros((PANEL, start), f32)] + pieces
    if end < n:
        pieces = pieces + [jnp.zeros((PANEL, n - end), f32)]
    inside = (lane >= start) & (lane < end)
    rows = jnp.where(inside, jnp.concatenate(pieces, axis=1), panel)
    out_ref[...] = jnp.where(lane < end, rows * jnp.sqrt(pivots), 0.0)
    if end < n:
        factors = (panel * pivots)[:, end:]
        lane_r = lax.broadcasted_iota(jnp.int32, (n - end, n), 1)
        old = jnp.where((lane_r >= start) & (lane_r < end), 0.0, state_ref[PANEL:, :])
        next_ref[...] = old - dot_f32(factors, rows, 0, 0)


def factor_calls(flags, part, other):
    n = part.shape[1] * 2
    rows = []
    state = None
    for start in range(0, n, PANEL):
        left = n - start - PANEL
        outs = [on_chip((PANEL, n), f32)]
        if left:
            outs.append(on_chip((left, n), f32))
        args = (flags, *held(part, other)) if start == 0 else held(state)
        got = pl.pallas_call(
            functools.partial(factor_kernel, start),
            in_specs=[SMEM, VMEM, VMEM] if start == 0 else [VMEM],
            out_specs=[VMEM] * len(outs),
            out_shape=outs,
            scratch_shapes=([pltpu.VMEM((n, n), f32)] if start == 0 else [])
            + [pltpu.VMEM((TILE * TILE, PANEL), f32)],
            compiler_params=PARAMS,
        )(*args)
        rows.append(got[0])
        if left:
            state = got[1]
    return rows


def finish_kernel(steps, flag_ref, part_ref, other_ref, image0_ref, image1_ref, *refs):
    count = len(refs) - 6
    inverse_refs, rest = refs[:count], refs[count:]
    out_ref, reduced_ref, right_ref, made_ref, sum_ref, sems = rest
    columns = out_ref.shape[1]
    half = columns // 2
    inverse = jnp.concatenate([ref[...] for ref in inverse_refs], axis=0)
    own_first = flag_ref[3] == 0
    part = jnp.concatenate([part_ref[:half, :], part_ref[half:, :]], axis=1)
    other = jnp.concatenate([other_ref[:half, :], other_ref[half:, :]], axis=1)
    gram = jnp.concatenate(
        [jnp.where(own_first, part, other), jnp.where(own_first, other, part)], axis=0
    )
    high, low = split2(inverse)
    right_ref[...] = jnp.concatenate([high, low, high], axis=1)
    right = right_ref[...]
    block = out_ref.shape[0] // steps
    copies = []

    def send(source, target):
        copies.append(pltpu.make_async_copy(source, target, sems.at[len(copies)]))
        copies[-1].start()

    def applied(i):
        ref, at = (image0_ref, i) if i < steps // 2 else (image1_ref, i - steps // 2)
        image = ref[at * block : (at + 1) * block, :]
        left = jnp.concatenate([image[:, :columns], image], axis=1)
        made_ref[i * block : (i + 1) * block, :] = matmul(left, right, 1, 1).astype(bf16)

    middle = dot_f32(inverse, gram, 1, 0)
    for i in range(steps - 1):
        applied(i)
    span = pl.ds(0, (steps - 1) * block)
    send(made_ref.at[span], out_ref.at[span])
    sum_ref[...] = dot_f32(middle, inverse, 1, 1)
    applied(steps - 1)
    span = pl.ds((steps - 1) * block, block)
    send(sum_ref, reduced_ref)
    send(made_ref.at[span], out_ref.at[span])
    for copy in copies:
        copy.wait()


def finish_call(flags, part, other, image0, image1, rows):
    count, columns = image0.shape[0] * 2, image0.shape[1] // 2
    steps = 4
    return pl.pallas_call(
        functools.partial(finish_kernel, steps),
        in_specs=[SMEM] + [VMEM] * (4 + len(rows)),
        out_specs=[HBM, HBM],
        out_shape=[
            jax.ShapeDtypeStruct((count, columns), bf16),
            jax.ShapeDtypeStruct((columns, columns), f32),
        ],
        scratch_shapes=[
            pltpu.VMEM((columns, 3 * columns), bf16),
            pltpu.VMEM((count, columns), bf16),
            pltpu.VMEM((columns, columns), f32),
            pltpu.SemaphoreType.DMA((3,)),
        ],
        compiler_params=PARAMS,
        name="finish",
    )(flags, *held(part, other, image0, image1, *rows))


AXES = ("gx", "gy", "gz")
PLANE = ("gx", "gy")


def swap(value, masks):
    depth = lax.axis_size("gz")
    pairs = [(i, i ^ masks[i // depth % 2]) for i in range(lax.axis_size(AXES))]
    return lax.ppermute(value, AXES, pairs)


def stages():
    depth = lax.axis_size("gz")
    plane, line = [], []
    mask = 2
    while mask < lax.axis_size(PLANE):
        plane.append(mask * depth)
        mask *= 2
    mask = 1
    while mask < depth:
        line.append(mask)
        mask *= 2
    bits = line[-1:] + plane + line[:-1]
    turned = list(bits)
    for k in range(0, len(bits) - 1, 2):
        turned[k], turned[k + 1] = bits[k + 1], bits[k]
    return list(zip(bits, turned))


def exchange(part, masks):
    got = swap(part, masks)
    return part + got


def trade(sent):
    depth = lax.axis_size("gz")
    return swap(sent, (depth, depth))


def halo_pair(first, second, axis):
    count = lax.axis_size(axis)
    got = []
    for start, layer in ((0, first), (1, second)):
        pairs = []
        for i in range(start, count - 1, 2):
            pairs += [(i, i + 1), (i + 1, i)]
        if pairs:
            got.append(lax.ppermute(layer, axis, pairs))
        else:
            got.append(jnp.zeros_like(layer))
    return got


def body(snapshots, sketch, velocity, viscosity):
    shape = snapshots.shape
    ncells = shape[0] * shape[1] * shape[2]
    for axis in ("gx", "gy", "gz"):
        ncells *= lax.axis_size(axis)
    scale = 1.0 / ncells
    flags = [lax.axis_index(axis) % 2 for axis in ("gx", "gy", "gz")]
    flags = jnp.stack(flags + [lax.axis_index(PLANE) % 2]).astype(jnp.int32)
    sketched, x1, x2, y1, y2, z1, z2, sent, kept, coefs = sketch_call(
        flags, snapshots, sketch, velocity, viscosity, scale
    )
    steps = stages()
    part = kept + trade(sent)
    for masks in steps:
        part = exchange(part, masks)
    other = trade(part)
    halos = halo_pair(x1, x2, "gx") + halo_pair(y1, y2, "gy")
    halos = halos + halo_pair(z1, z2, "gz")
    image0, image1, sent, kept = operator_calls(flags, sketched, halos, coefs, scale)
    i_part = kept + trade(sent)
    turn = [3, 0, 1, 2] if len(steps) == 4 else range(len(steps))
    for stage in turn:
        i_part = exchange(i_part, steps[stage])
    i_other = trade(i_part)
    rows = factor_calls(flags, part, other)
    applied, reduced = finish_call(flags, i_part, i_other, image0, image1, rows)
    return applied.reshape(shape), reduced


def solution(mesh):
    in_specs = (P("gx", "gy", "gz", None), P(), P(None, "gx", "gy", "gz"), P("gx", "gy", "gz"))
    out_specs = (P("gx", "gy", "gz", None), P())
    return jax.shard_map(body, mesh=mesh, in_specs=in_specs, out_specs=out_specs, check_vma=False)
```

profile of v0, /device:TPU:0, one launch (start us, length us, event | category | flops | bytes accessed | tf_op | source)
XLA Modules:
  0.0 68.9 jit_solution(1142492960867837015)
XLA Ops:
  0.7 0.1 pad_add_fusion.flag_ref.refs_0_
  0.7 4.6 %sketch.1 = (bf16[8,16,16,256]{3,2,1,0:T(8,128)(2,1)S(1)}, bf16[16,16,256]{2,1,0:T(8,128)(2,1)S(1)}, bf16[16,16,256]{2,1,0:T(8,128)(2,1)}, bf16[8,16,256]{2,1,0:...) custom-call(s32[4]{0:T(128)S(1)} %pad_add_fusion.flag_ref.refs_0_, ...), custom_call_target="tpu_custom_call" | custom-call | tf_op jit(solution)/shard_map/sketch/pallas_call | solution.py:140
  5.4 3.1 %collective-permute-start = (bf16[16,16,256]{2,1,0:T(8,128)(2,1)S(1)}, bf16[16,16,256]{2,1,0:T(8,128)(2,1)S(1)}, u32[]{:S(2)}, u32[]{:S(2)}) collective-permute-start(bf16[16,16,256]{2,1,0:T(8,128)(2,1)S(1)} %get-tuple-element.25), channel_id=1, source_target_pairs={{0,16},{16,0},{1,17},{17,1},{2,18},{18,2},{3,19},{19,3},{4,20},{20... | collective-permute-start | bytes 393224 | tf_op jit(solution)/shard_map/ppermute | solution.py:524
  8.4 0.7 collective-permute-start.2
  9.1 1.6 %collective-permute-start.3 = (bf16[8,16,256]{2,1,0:T(8,128)(2,1)S(1)}, bf16[8,16,256]{2,1,0:T(8,128)(2,1)S(1)}, u32[]{:S(2)}, u32[]{:S(2)}) collective-permute-start(bf16[8,16,256]{2,1,0:T(8,128)(2,1)S(1)} %get-tuple-element.28), channel_id=1, source_target_pairs={{0,1},{1,0},{2,3},{3,2},{4,5},{5,4},{6,7},{7,6},{8,9},{9,8},{10,11... | collective-permute-start | bytes 196616 | tf_op jit(solution)/shard_map/ppermute | solution.py:524
  10.7 0.7 collective-permute-start.4
  11.4 2.0 %collective-permute-done.3.z1_ref = bf16[8,16,256]{2,1,0:T(8,128)(2,1)S(1)} collective-permute-done((bf16[8,16,256]{2,1,0:T(8,128)(2,1)S(1)}, bf16[8,16,256]{2,1,0:T(8,128)(2,1)S(1)}, u32[]{:S(2)}, u32[]{:S(2)}) %collective-permute-start.3) | collective-permute-done | bytes 65568 | tf_op jit(solution)/shard_map/ppermute | solution.py:524
  13.4 2.1 %operator0.1 = (bf16[1024,512]{1,0:T(8,128)(2,1)S(1)}, f32[256,256]{1,0:T(8,128)S(1)}) custom-call(s32[4]{0:T(128)S(1)} %pad_add_fusion.flag_ref.refs_0_, bf16[8,16,16,256]{3,2,1,0:T(8,128)(2,1)S(1)} %get-tuple-element.24.s_ref, bf16[16,16,256]{2,1,0:T(8,128)(2,1)S(1)} %collective-permute-done.x1_ref, bf16[16,16,256]{2,1,0:T(8,128)(2,1)S(1)} %broadcast_in_dim.3.x2_ref, ...), custom_call_target="tpu_custom_call" | custom-call | tf_op jit(solution)/shard_map/operator0/pallas_call | solution.py:256
  15.5 2.1 %operator1.1 = (bf16[1024,512]{1,0:T(8,128)(2,1)S(1)}, f32[256,128]{1,0:T(8,128)S(1)}, f32[256,128]{1,0:T(8,128)S(1)}) custom-call(s32[4]{0:T(128)S(1)} %pad_add_fusion.flag_ref.refs_0_, bf16[8,16,16,256]{3,2,1,0:T(8,128)(2,1)S(1)} %get-tuple-element.24.s_ref, bf16[16,16,256]{2,1,0:T(8,128)(2,1)S(1)} %collective-permute-done.x1_ref, ...), custom_call_target="tpu_custom_call" | custom-call | tf_op jit(solution)/shard_map/operator1/pallas_call | solution.py:264
  17.7 1.8 %collective-permute-start.5 = (f32[256,128]{1,0:T(8,128)S(1)}, f32[256,128]{1,0:T(8,128)S(1)}, u32[]{:S(2)}, u32[]{:S(2)}) collective-permute-start(f32[256,128]{1,0:T(8,128)S(1)} %get-tuple-element.33), channel_id=1, source_target_pairs={{0,4},{1,5},{2,6},{3,7},{4,0},{5,1},{6,2},{7,3},{8,12},{9,13},{10,... | collective-permute-start | bytes 393224 | tf_op jit(solution)/shard_map/ppermute | solution.py:485
  19.4 1.0 %collective-permute-done.5 = f32[256,128]{1,0:T(8,128)S(1)} collective-permute-done((f32[256,128]{1,0:T(8,128)S(1)}, f32[256,128]{1,0:T(8,128)S(1)}, u32[]{:S(2)}, u32[]{:S(2)}) %collective-permute-start.5) | collective-permute-done | bytes 131104 | tf_op jit(solution)/shard_map/ppermute | solution.py:485
  20.4 4.7 %collective-permute-start.6 = (f32[256,128]{1,0:T(8,128)S(1)}, f32[256,128]{1,0:T(8,128)S(1)}, u32[]{:S(2)}, u32[]{:S(2)}) collective-permute-start(f32[256,128]{1,0:T(8,128)S(1)} %add.51), channel_id=1, source_target_pairs={{0,1},{1,0},{2,3},{3,2},{4,20},{5,21},{6,22},{7,23},{8,9},{9,8},{1... | collective-permute-start | bytes 393224 | tf_op jit(solution)/shard_map/ppermute | solution.py:485
  25.1 2.9 %collective-permute-done.6 = f32[256,128]{1,0:T(8,128)S(1)} collective-permute-done((f32[256,128]{1,0:T(8,128)S(1)}, f32[256,128]{1,0:T(8,128)S(1)}, u32[]{:S(2)}, u32[]{:S(2)}) %collective-permute-start.6) | collective-permute-done | bytes 131104 | tf_op jit(solution)/shard_map/ppermute | solution.py:485
  28.1 3.3 %collective-permute-start.7 = (f32[256,128]{1,0:T(8,128)S(1)}, f32[256,128]{1,0:T(8,128)S(1)}, u32[]{:S(2)}, u32[]{:S(2)}) collective-permute-start(f32[256,128]{1,0:T(8,128)S(1)} %add.52), channel_id=1, source_target_pairs={{0,2},{1,3},{2,0},{3,1},{4,12},{5,13},{6,14},{7,15},{8,10},{9,11},... | collective-permute-start | bytes 393224 | tf_op jit(solution)/shard_map/ppermute | solution.py:485
  31.3 0.1 collective-permute-start.12
  31.4 6.7 %collective-permute-done.12 = f32[192,128]{1,0:T(8,128)S(1)} collective-permute-done((f32[192,128]{1,0:T(8,128)S(1)}, f32[192,128]{1,0:T(8,128)S(1)}, u32[]{:S(2)}, u32[]{:S(2)}) %collective-permute-start.12) | collective-permute-done | bytes 98336 | tf_op jit(solution)/shard_map/ppermute | solution.py:485
  38.1 5.8 %collective-permute-start.13 = (f32[192,128]{1,0:T(8,128)S(1)}, f32[192,128]{1,0:T(8,128)S(1)}, u32[]{:S(2)}, u32[]{:S(2)}) collective-permute-start(f32[192,128]{1,0:T(8,128)S(1)} %add.57), channel_id=1, source_target_pairs={{0,8},{1,9},{2,10},{3,11},{4,6},{5,7},{6,4},{7,5},{8,0},{9,1},{10,... | collective-permute-start | bytes 294920 | tf_op jit(solution)/shard_map/ppermute | solution.py:485
  44.0 0.1 collective-permute-start.8
  44.1 2.5 %collective-permute-done.13 = f32[192,128]{1,0:T(8,128)S(1)} collective-permute-done((f32[192,128]{1,0:T(8,128)S(1)}, f32[192,128]{1,0:T(8,128)S(1)}, u32[]{:S(2)}, u32[]{:S(2)}) %collective-permute-start.13) | collective-permute-done | bytes 98336 | tf_op jit(solution)/shard_map/ppermute | solution.py:485
  46.6 0.6 collective-permute-start.14
  47.2 1.9 %collective-permute-done.8 = f32[256,128]{1,0:T(8,128)S(1)} collective-permute-done((f32[256,128]{1,0:T(8,128)S(1)}, f32[256,128]{1,0:T(8,128)S(1)}, u32[]{:S(2)}, u32[]{:S(2)}) %collective-permute-start.8) | collective-permute-done | bytes 131104 | tf_op jit(solution)/shard_map/ppermute | solution.py:485
  49.1 0.6 collective-permute-start.9
  49.6 1.6 %collective-permute-done.14 = f32[192,128]{1,0:T(8,128)S(1)} collective-permute-done((f32[192,128]{1,0:T(8,128)S(1)}, f32[192,128]{1,0:T(8,128)S(1)}, u32[]{:S(2)}, u32[]{:S(2)}) %collective-permute-start.14) | collective-permute-done | bytes 98336 | tf_op jit(solution)/shard_map/ppermute | solution.py:485
  51.4 2.7 %collective-permute-done.9 = f32[256,128]{1,0:T(8,128)S(1)} collective-permute-done((f32[256,128]{1,0:T(8,128)S(1)}, f32[256,128]{1,0:T(8,128)S(1)}, u32[]{:S(2)}, u32[]{:S(2)}) %collective-permute-start.9) | collective-permute-done | bytes 131104 | tf_op jit(solution)/shard_map/ppermute | solution.py:485
  54.1 0.1 collective-permute-start.10
  54.2 1.8 %collective-permute-done.15 = f32[192,128]{1,0:T(8,128)S(1)} collective-permute-done((f32[192,128]{1,0:T(8,128)S(1)}, f32[192,128]{1,0:T(8,128)S(1)}, u32[]{:S(2)}, u32[]{:S(2)}) %collective-permute-start.15) | collective-permute-done | bytes 98336 | tf_op jit(solution)/shard_map/ppermute | solution.py:485
  56.1 1.3 %collective-permute-done.16.refs_2_ = f32[192,128]{1,0:T(8,128)S(1)} collective-permute-done((f32[192,128]{1,0:T(8,128)S(1)}, f32[192,128]{1,0:T(8,128)S(1)}, u32[]{:S(2)}, u32[]{:S(2)}) %collective-permute-start.16) | collective-permute-done | bytes 98336 | tf_op jit(solution)/shard_map/ppermute | solution.py:485
  57.4 2.7 %shard_map.59 = (f32[64,256]{1,0:T(8,128)S(1)}, f32[192,256]{1,0:T(8,128)S(1)}) custom-call(s32[4]{0:T(128)S(1)} %pad_add_fusion.flag_ref.refs_0_, f32[192,128]{1,0:T(8,128)S(1)} %add.60.refs_1_, f32[192,128]{1,0:T(8,128)S(1)} %collective-permute-done.16.refs_2_), custom_call_target="tpu_custom_call" | custom-call | tf_op jit(solution)/shard_map/pallas_call | solution.py:398
  60.1 2.1 %shard_map.60 = (f32[64,256]{1,0:T(8,128)S(1)}, f32[128,256]{1,0:T(8,128)S(1)}) custom-call(f32[192,256]{1,0:T(8,128)S(1)} %get-tuple-element.39.refs_0_), custom_call_target="tpu_custom_call" | custom-call | tf_op jit(solution)/shard_map/pallas_call | solution.py:398
  62.2 2.1 %shard_map.61 = (f32[64,256]{1,0:T(8,128)S(1)}, f32[64,256]{1,0:T(8,128)S(1)}) custom-call(f32[128,256]{1,0:T(8,128)S(1)} %get-tuple-element.41.refs_0_), custom_call_target="tpu_custom_call" | custom-call | tf_op jit(solution)/shard_map/pallas_call | solution.py:398
  64.3 1.8 %shard_map.62.refs_3_ = f32[64,256]{1,0:T(8,128)S(1)} custom-call(f32[64,256]{1,0:T(8,128)S(1)} %get-tuple-element.43.refs_0_), custom_call_target="tpu_custom_call" | custom-call | tf_op jit(solution)/shard_map/pallas_call | solution.py:398
  66.2 2.8 %finish.1 = (bf16[2048,256]{1,0:T(8,128)(2,1)}, f32[256,256]{1,0:T(8,128)}) custom-call(s32[4]{0:T(128)S(1)} %pad_add_fusion.flag_ref.refs_0_, f32[256,128]{1,0:T(8,128)S(1)} %add.55.part_ref, f32[256,128]{1,0:T(8,128)S(1)} %collective-permute-done.10.other_ref, bf16[1024,512]{1,0:T(8,128)(2,1)S(1)} %get-tuple-element.34.image0_ref, ...), custom_call_target="tpu_custom_call" | custom-call | tf_op jit(solution)/shard_map/finish/pallas_call | solution.py:459
  (22 shorter events, 0.3 us)
Async XLA Ops:
  5.4 8.1 %collective-permute-start = (bf16[16,16,256]{2,1,0:T(8,128)(2,1)S(1)}, bf16[16,16,256]{2,1,0:T(8,128)(2,1)S(1)}, u32[]{:S(2)}, u32[]{:S(2)}) collective-permute-start(bf16[16,16,256]{2,1,0:T(8,128)(2,1)S(1)} %get-tuple-element.25), channel_id=1, source_target_pairs={{0,16},{16,0},{1,17},{17,1},{2,18},{18,2},{3,19},{19,3},{4,20},{20... | collective-permute-start | bytes 393224 | tf_op jit(solution)/shard_map/ppermute | solution.py:524
  8.4 3.0 %collective-permute-start.1 = (bf16[8,16,256]{2,1,0:T(8,128)(2,1)S(1)}, bf16[8,16,256]{2,1,0:T(8,128)(2,1)S(1)}, u32[]{:S(2)}, u32[]{:S(2)}) collective-permute-start(bf16[8,16,256]{2,1,0:T(8,128)(2,1)S(1)} %get-tuple-element.26), channel_id=1, source_target_pairs={{0,4},{4,0},{8,12},{12,8},{1,5},{5,1},{9,13},{13,9},{2,6},{6,2},{1... | collective-permute-start | bytes 196616 | tf_op jit(solution)/shard_map/ppermute | solution.py:524
  8.4 3.0 %collective-permute-start.2 = (bf16[8,16,256]{2,1,0:T(8,128)(2,1)S(1)}, bf16[8,16,256]{2,1,0:T(8,128)(2,1)S(1)}, u32[]{:S(2)}, u32[]{:S(2)}) collective-permute-start(bf16[8,16,256]{2,1,0:T(8,128)(2,1)S(1)} %get-tuple-element.27), channel_id=1, source_target_pairs={{4,8},{8,4},{5,9},{9,5},{6,10},{10,6},{7,11},{11,7},{20,24},{24,20... | collective-permute-start | bytes 196616 | tf_op jit(solution)/shard_map/ppermute | solution.py:524
  9.1 4.3 %collective-permute-start.3 = (bf16[8,16,256]{2,1,0:T(8,128)(2,1)S(1)}, bf16[8,16,256]{2,1,0:T(8,128)(2,1)S(1)}, u32[]{:S(2)}, u32[]{:S(2)}) collective-permute-start(bf16[8,16,256]{2,1,0:T(8,128)(2,1)S(1)} %get-tuple-element.28), channel_id=1, source_target_pairs={{0,1},{1,0},{2,3},{3,2},{4,5},{5,4},{6,7},{7,6},{8,9},{9,8},{10,11... | collective-permute-start | bytes 196616 | tf_op jit(solution)/shard_map/ppermute | solution.py:524
  10.7 2.7 %collective-permute-start.4 = (bf16[8,16,256]{2,1,0:T(8,128)(2,1)S(1)}, bf16[8,16,256]{2,1,0:T(8,128)(2,1)S(1)}, u32[]{:S(2)}, u32[]{:S(2)}) collective-permute-start(bf16[8,16,256]{2,1,0:T(8,128)(2,1)S(1)} %get-tuple-element.29), channel_id=1, source_target_pairs={{1,2},{2,1},{5,6},{6,5},{9,10},{10,9},{13,14},{14,13},{17,18},{18,... | collective-permute-start | bytes 196616 | tf_op jit(solution)/shard_map/ppermute | solution.py:524
  17.7 2.8 %collective-permute-start.5 = (f32[256,128]{1,0:T(8,128)S(1)}, f32[256,128]{1,0:T(8,128)S(1)}, u32[]{:S(2)}, u32[]{:S(2)}) collective-permute-start(f32[256,128]{1,0:T(8,128)S(1)} %get-tuple-element.33), channel_id=1, source_target_pairs={{0,4},{1,5},{2,6},{3,7},{4,0},{5,1},{6,2},{7,3},{8,12},{9,13},{10,... | collective-permute-start | bytes 393224 | tf_op jit(solution)/shard_map/ppermute | solution.py:485
  20.4 7.6 %collective-permute-start.6 = (f32[256,128]{1,0:T(8,128)S(1)}, f32[256,128]{1,0:T(8,128)S(1)}, u32[]{:S(2)}, u32[]{:S(2)}) collective-permute-start(f32[256,128]{1,0:T(8,128)S(1)} %add.51), channel_id=1, source_target_pairs={{0,1},{1,0},{2,3},{3,2},{4,20},{5,21},{6,22},{7,23},{8,9},{9,8},{1... | collective-permute-start | bytes 393224 | tf_op jit(solution)/shard_map/ppermute | solution.py:485
  25.1 6.2 %collective-permute-start.11 = (f32[192,128]{1,0:T(8,128)S(1)}, f32[192,128]{1,0:T(8,128)S(1)}, u32[]{:S(2)}, u32[]{:S(2)}) collective-permute-start(f32[192,128]{1,0:T(8,128)S(1)} %get-tuple-element.37), channel_id=1, source_target_pairs={{0,4},{1,5},{2,6},{3,7},{4,0},{5,1},{6,2},{7,3},{8,12},{9,13},{10,... | collective-permute-start | bytes 294920 | tf_op jit(solution)/shard_map/ppermute | solution.py:485
  28.1 15.9 %collective-permute-start.7 = (f32[256,128]{1,0:T(8,128)S(1)}, f32[256,128]{1,0:T(8,128)S(1)}, u32[]{:S(2)}, u32[]{:S(2)}) collective-permute-start(f32[256,128]{1,0:T(8,128)S(1)} %add.52), channel_id=1, source_target_pairs={{0,2},{1,3},{2,0},{3,1},{4,12},{5,13},{6,14},{7,15},{8,10},{9,11},... | collective-permute-start | bytes 393224 | tf_op jit(solution)/shard_map/ppermute | solution.py:485
  31.3 6.8 %collective-permute-start.12 = (f32[192,128]{1,0:T(8,128)S(1)}, f32[192,128]{1,0:T(8,128)S(1)}, u32[]{:S(2)}, u32[]{:S(2)}) collective-permute-start(f32[192,128]{1,0:T(8,128)S(1)} %add.56), channel_id=1, source_target_pairs={{0,2},{1,3},{2,0},{3,1},{4,12},{5,13},{6,14},{7,15},{8,10},{9,11},... | collective-permute-start | bytes 294920 | tf_op jit(solution)/shard_map/ppermute | solution.py:485
  38.1 8.4 %collective-permute-start.13 = (f32[192,128]{1,0:T(8,128)S(1)}, f32[192,128]{1,0:T(8,128)S(1)}, u32[]{:S(2)}, u32[]{:S(2)}) collective-permute-start(f32[192,128]{1,0:T(8,128)S(1)} %add.57), channel_id=1, source_target_pairs={{0,8},{1,9},{2,10},{3,11},{4,6},{5,7},{6,4},{7,5},{8,0},{9,1},{10,... | collective-permute-start | bytes 294920 | tf_op jit(solution)/shard_map/ppermute | solution.py:485
  44.0 5.0 %collective-permute-start.8 = (f32[256,128]{1,0:T(8,128)S(1)}, f32[256,128]{1,0:T(8,128)S(1)}, u32[]{:S(2)}, u32[]{:S(2)}) collective-permute-start(f32[256,128]{1,0:T(8,128)S(1)} %add.53), channel_id=1, source_target_pairs={{0,8},{1,9},{2,10},{3,11},{4,6},{5,7},{6,4},{7,5},{8,0},{9,1},{10,... | collective-permute-start | bytes 393224 | tf_op jit(solution)/shard_map/ppermute | solution.py:485
  46.6 4.7 %collective-permute-start.14 = (f32[192,128]{1,0:T(8,128)S(1)}, f32[192,128]{1,0:T(8,128)S(1)}, u32[]{:S(2)}, u32[]{:S(2)}) collective-permute-start(f32[192,128]{1,0:T(8,128)S(1)} %add.58), channel_id=1, source_target_pairs={{0,16},{1,17},{2,18},{3,19},{4,5},{5,4},{6,7},{7,6},{8,24},{9,25},... | collective-permute-start | bytes 294920 | tf_op jit(solution)/shard_map/ppermute | solution.py:485
  49.1 5.0 %collective-permute-start.9 = (f32[256,128]{1,0:T(8,128)S(1)}, f32[256,128]{1,0:T(8,128)S(1)}, u32[]{:S(2)}, u32[]{:S(2)}) collective-permute-start(f32[256,128]{1,0:T(8,128)S(1)} %add.54), channel_id=1, source_target_pairs={{0,16},{1,17},{2,18},{3,19},{4,5},{5,4},{6,7},{7,6},{8,24},{9,25},... | collective-permute-start | bytes 393224 | tf_op jit(solution)/shard_map/ppermute | solution.py:485
  51.3 4.7 %collective-permute-start.15 = (f32[192,128]{1,0:T(8,128)S(1)}, f32[192,128]{1,0:T(8,128)S(1)}, u32[]{:S(2)}, u32[]{:S(2)}) collective-permute-start(f32[192,128]{1,0:T(8,128)S(1)} %add.59), channel_id=1, source_target_pairs={{0,1},{1,0},{2,3},{3,2},{4,20},{5,21},{6,22},{7,23},{8,9},{9,8},{1... | collective-permute-start | bytes 294920 | tf_op jit(solution)/shard_map/ppermute | solution.py:485
  54.1 12.0 %collective-permute-start.10 = (f32[256,128]{1,0:T(8,128)S(1)}, f32[256,128]{1,0:T(8,128)S(1)}, u32[]{:S(2)}, u32[]{:S(2)}) collective-permute-start(f32[256,128]{1,0:T(8,128)S(1)} %add.55.part_ref), channel_id=1, source_target_pairs={{0,4},{1,5},{2,6},{3,7},{4,0},{5,1},{6,2},{7,3},{8,12},{9,13},{10,... | collective-permute-start | bytes 393224 | tf_op jit(solution)/shard_map/ppermute | solution.py:485
  56.0 1.4 %collective-permute-start.16 = (f32[192,128]{1,0:T(8,128)S(1)}, f32[192,128]{1,0:T(8,128)S(1)}, u32[]{:S(2)}, u32[]{:S(2)}) collective-permute-start(f32[192,128]{1,0:T(8,128)S(1)} %add.60.refs_1_), channel_id=1, source_target_pairs={{0,4},{1,5},{2,6},{3,7},{4,0},{5,1},{6,2},{7,3},{8,12},{9,13},{10,... | collective-permute-start | bytes 294920 | tf_op jit(solution)/shard_map/ppermute | solution.py:485
where the time goes:
time: 69.1 us; the launch traced here: 68.9 us
  waiting for transfers between devices  24.5 us (35%)
  starting transfers between devices  23.1 us (33%)
  Pallas kernels  20.3 us (29%)
  between operations  0.81 us (1%)
    ppermute x12, waiting for transfers between devices, swap(): return lax.ppermute(value, AXES, pairs)  22.5 us
    ppermute x12, starting transfers between devices, swap(): return lax.ppermute(value, AXES, pairs)  17.1 us
    pallas_call x4, Pallas kernels, factor_calls(): pl.pallas_call(functools.partial(factor_kernel, start), in_specs=[SMEM, V...  8.74 us
    ppermute x5, starting transfers between devices, halo_pair(): got.append(lax.ppermute(layer, axis, pairs))  6.01 us
    pallas_call x1, Pallas kernels, sketch_call(): pl.pallas_call(functools.partial(sketch_kernel, scale, steps), in_specs=[...  4.61 us
    pallas_call x1, Pallas kernels, finish_call(): pl.pallas_call(functools.partial(finish_kernel, steps), in_specs=[SMEM] +...  2.75 us
    pallas_call x1, Pallas kernels, operator_calls(): pl.pallas_call(functools.partial(operator_kernel, scale, range(half, cell...  2.11 us
    pallas_call x1, Pallas kernels, operator_calls(): pl.pallas_call(functools.partial(operator_kernel, scale, range(half)), in...  2.1 us
  transfers between devices with their start and end apart: 17, of which 10 were waited for; matrix products, arithmetic and copies ran while one was open for 0% of the time, Pallas kernels for 13%

commit v1 on v0

--- a/solution.py
+++ b/solution.py
@@ -136,7 +136,7 @@
 def sketch_call(flags, snapshots, sketch, velocity, viscosity, scale):
     cells_x, cells_y, cells_z, columns = snapshots.shape
     half = columns // 2
-    steps = 2
+    steps = 1
     return pl.pallas_call(
         functools.partial(sketch_kernel, scale, steps),
         in_specs=[SMEM] + [HBM] * 4,
@@ -181,7 +181,7 @@
     *refs,
 ):
     cells_x, cells_y, cells_z, columns = s_ref.shape
-    first = planes[0]
+    first, last = planes[0], planes[-1]
     even = [flag_ref[k] == 0 for k in range(3)]
     if first == 0:
         image_ref, total_ref = refs
@@ -225,28 +225,19 @@
             at = ((x - first) * cells_y + y) * cells_z
             image_ref[at : at + cells_z, :columns] = high
             image_ref[at : at + cells_z, columns:] = low
-        plane = s_ref[x]
-        at = (x - first) * cells_y * cells_z
-        high = image_ref[at : at + cells_y * cells_z, :columns]
-        low = image_ref[at : at + cells_y * cells_z, columns:]
-        base = plane.reshape(-1, columns)
-        part = matmul(
-            jnp.concatenate([base, base], axis=0), jnp.concatenate([high, low], axis=0), 0, 0
-        )
-        if x > first:
-            part = total_ref[...] + part
-        elif first > 0:
-            part = sum_ref[...] + part
-        if x < cells_x - 1:
-            total_ref[...] = part
-        else:
-            total_ref[...] = part * scale
-            size = columns // 2
-            mine = pl.multiple_of(flag_ref[3] * size, size)
-            other = pl.multiple_of((1 - flag_ref[3]) * size, size)
-            for at in (0, size):
-                kept_ref[at : at + size, :] = total_ref[pl.ds(mine, size), at : at + size]
-                sent_ref[at : at + size, :] = total_ref[pl.ds(other, size), at : at + size]
+    base = s_ref[first : last + 1].reshape(-1, columns)
+    high, low = image_ref[:, :columns], image_ref[:, columns:]
+    part = matmul(jnp.concatenate([base, base], axis=0), jnp.concatenate([high, low], axis=0), 0, 0)
+    if first == 0:
+        total_ref[...] = part
+    else:
+        total_ref[...] = (sum_ref[...] + part) * scale
+        size = columns // 2
+        mine = pl.multiple_of(flag_ref[3] * size, size)
+        other = pl.multiple_of((1 - flag_ref[3]) * size, size)
+        for at in (0, size):
+            kept_ref[at : at + size, :] = total_ref[pl.ds(mine, size), at : at + size]
+            sent_ref[at : at + size, :] = total_ref[pl.ds(other, size), at : at + size]
 
 
 def operator_calls(flags, sketched, halos, coefs, scale):
@@ -401,7 +392,7 @@
             out_specs=[VMEM] * len(outs),
             out_shape=outs,
             scratch_shapes=([pltpu.VMEM((n, n), f32)] if start == 0 else [])
-            + [pltpu.VMEM((TILE * TILE, PANEL), f32)],
+            + [pltpu.VMEM((TILE * TILE + TILE, PANEL), f32)],
             compiler_params=PARAMS,
         )(*args)
         rows.append(got[0])

time: 69.1 us -> 68.6 us (level)
  no operation moved by 1% of the time
where the time goes in v1:
time: 68.6 us; the launch traced here: 68.5 us
  waiting for transfers between devices  24.5 us (36%)
  starting transfers between devices  23.1 us (34%)
  Pallas kernels  19.9 us (29%)
  between operations  0.81 us (1%)
    ppermute x12, waiting for transfers between devices, swap(): return lax.ppermute(value, AXES, pairs)  22.4 us
    ppermute x12, starting transfers between devices, swap(): return lax.ppermute(value, AXES, pairs)  17.1 us
    pallas_call x4, Pallas kernels, factor_calls(): pl.pallas_call(functools.partial(factor_kernel, start), in_specs=[SMEM, V...  8.73 us
    ppermute x5, starting transfers between devices, halo_pair(): got.append(lax.ppermute(layer, axis, pairs))  6.01 us
    pallas_call x1, Pallas kernels, sketch_call(): pl.pallas_call(functools.partial(sketch_kernel, scale, steps), in_specs=[...  4.15 us
    pallas_call x1, Pallas kernels, finish_call(): pl.pallas_call(functools.partial(finish_kernel, steps), in_specs=[SMEM] +...  2.75 us
    pallas_call x1, Pallas kernels, operator_calls(): pl.pallas_call(functools.partial(operator_kernel, scale, range(half)), in...  2.11 us
    pallas_call x1, Pallas kernels, operator_calls(): pl.pallas_call(functools.partial(operator_kernel, scale, range(half, cell...  2.11 us
  transfers between devices with their start and end apart: 17, of which 10 were waited for; matrix products, arithmetic and copies ran while one was open for 0% of the time, Pallas kernels for 13%

profile of v1, /device:TPU:0, one launch (start us, length us, event | category | flops | bytes accessed | tf_op | source)
XLA Modules:
  0.0 68.5 jit_solution(11523097995917337211)
XLA Ops:
  0.7 0.1 pad_add_fusion.flag_ref.refs_0_
  0.7 4.2 %sketch.1 = (bf16[8,16,16,256]{3,2,1,0:T(8,128)(2,1)S(1)}, bf16[16,16,256]{2,1,0:T(8,128)(2,1)S(1)}, bf16[16,16,256]{2,1,0:T(8,128)(2,1)}, bf16[8,16,256]{2,1,0:...) custom-call(s32[4]{0:T(128)S(1)} %pad_add_fusion.flag_ref.refs_0_, ...), custom_call_target="tpu_custom_call" | custom-call | tf_op jit(solution)/shard_map/sketch/pallas_call | solution.py:140
  4.9 3.1 %collective-permute-start = (bf16[16,16,256]{2,1,0:T(8,128)(2,1)S(1)}, bf16[16,16,256]{2,1,0:T(8,128)(2,1)S(1)}, u32[]{:S(2)}, u32[]{:S(2)}) collective-permute-start(bf16[16,16,256]{2,1,0:T(8,128)(2,1)S(1)} %get-tuple-element.25), channel_id=1, source_target_pairs={{0,16},{16,0},{1,17},{17,1},{2,18},{18,2},{3,19},{19,3},{4,20},{20... | collective-permute-start | bytes 393224 | tf_op jit(solution)/shard_map/ppermute | solution.py:515
  8.0 0.7 collective-permute-start.2
  8.6 1.6 %collective-permute-start.3 = (bf16[8,16,256]{2,1,0:T(8,128)(2,1)S(1)}, bf16[8,16,256]{2,1,0:T(8,128)(2,1)S(1)}, u32[]{:S(2)}, u32[]{:S(2)}) collective-permute-start(bf16[8,16,256]{2,1,0:T(8,128)(2,1)S(1)} %get-tuple-element.28), channel_id=1, source_target_pairs={{0,1},{1,0},{2,3},{3,2},{4,5},{5,4},{6,7},{7,6},{8,9},{9,8},{10,11... | collective-permute-start | bytes 196616 | tf_op jit(solution)/shard_map/ppermute | solution.py:515
  10.3 0.7 collective-permute-start.4
  10.9 2.0 %collective-permute-done.3.z1_ref = bf16[8,16,256]{2,1,0:T(8,128)(2,1)S(1)} collective-permute-done((bf16[8,16,256]{2,1,0:T(8,128)(2,1)S(1)}, bf16[8,16,256]{2,1,0:T(8,128)(2,1)S(1)}, u32[]{:S(2)}, u32[]{:S(2)}) %collective-permute-start.3) | collective-permute-done | bytes 65568 | tf_op jit(solution)/shard_map/ppermute | solution.py:515
  13.0 2.1 %operator0.1 = (bf16[1024,512]{1,0:T(8,128)(2,1)S(1)}, f32[256,256]{1,0:T(8,128)S(1)}) custom-call(s32[4]{0:T(128)S(1)} %pad_add_fusion.flag_ref.refs_0_, bf16[8,16,16,256]{3,2,1,0:T(8,128)(2,1)S(1)} %get-tuple-element.24.s_ref, bf16[16,16,256]{2,1,0:T(8,128)(2,1)S(1)} %collective-permute-done.x1_ref, bf16[16,16,256]{2,1,0:T(8,128)(2,1)S(1)} %broadcast_in_dim.3.x2_ref, ...), custom_call_target="tpu_custom_call" | custom-call | tf_op jit(solution)/shard_map/operator0/pallas_call | solution.py:247
  15.1 2.1 %operator1.1 = (bf16[1024,512]{1,0:T(8,128)(2,1)S(1)}, f32[256,128]{1,0:T(8,128)S(1)}, f32[256,128]{1,0:T(8,128)S(1)}) custom-call(s32[4]{0:T(128)S(1)} %pad_add_fusion.flag_ref.refs_0_, bf16[8,16,16,256]{3,2,1,0:T(8,128)(2,1)S(1)} %get-tuple-element.24.s_ref, bf16[16,16,256]{2,1,0:T(8,128)(2,1)S(1)} %collective-permute-done.x1_ref, ...), custom_call_target="tpu_custom_call" | custom-call | tf_op jit(solution)/shard_map/operator1/pallas_call | solution.py:255
  17.2 1.8 %collective-permute-start.5 = (f32[256,128]{1,0:T(8,128)S(1)}, f32[256,128]{1,0:T(8,128)S(1)}, u32[]{:S(2)}, u32[]{:S(2)}) collective-permute-start(f32[256,128]{1,0:T(8,128)S(1)} %get-tuple-element.33), channel_id=1, source_target_pairs={{0,4},{1,5},{2,6},{3,7},{4,0},{5,1},{6,2},{7,3},{8,12},{9,13},{10,... | collective-permute-start | bytes 393224 | tf_op jit(solution)/shard_map/ppermute | solution.py:476
  19.0 1.0 %collective-permute-done.5 = f32[256,128]{1,0:T(8,128)S(1)} collective-permute-done((f32[256,128]{1,0:T(8,128)S(1)}, f32[256,128]{1,0:T(8,128)S(1)}, u32[]{:S(2)}, u32[]{:S(2)}) %collective-permute-start.5) | collective-permute-done | bytes 131104 | tf_op jit(solution)/shard_map/ppermute | solution.py:476
  20.0 4.7 %collective-permute-start.6 = (f32[256,128]{1,0:T(8,128)S(1)}, f32[256,128]{1,0:T(8,128)S(1)}, u32[]{:S(2)}, u32[]{:S(2)}) collective-permute-start(f32[256,128]{1,0:T(8,128)S(1)} %add.51), channel_id=1, source_target_pairs={{0,1},{1,0},{2,3},{3,2},{4,20},{5,21},{6,22},{7,23},{8,9},{9,8},{1... | collective-permute-start | bytes 393224 | tf_op jit(solution)/shard_map/ppermute | solution.py:476
  24.6 2.9 %collective-permute-done.6 = f32[256,128]{1,0:T(8,128)S(1)} collective-permute-done((f32[256,128]{1,0:T(8,128)S(1)}, f32[256,128]{1,0:T(8,128)S(1)}, u32[]{:S(2)}, u32[]{:S(2)}) %collective-permute-start.6) | collective-permute-done | bytes 131104 | tf_op jit(solution)/shard_map/ppermute | solution.py:476
  27.6 3.3 %collective-permute-start.7 = (f32[256,128]{1,0:T(8,128)S(1)}, f32[256,128]{1,0:T(8,128)S(1)}, u32[]{:S(2)}, u32[]{:S(2)}) collective-permute-start(f32[256,128]{1,0:T(8,128)S(1)} %add.52), channel_id=1, source_target_pairs={{0,2},{1,3},{2,0},{3,1},{4,12},{5,13},{6,14},{7,15},{8,10},{9,11},... | collective-permute-start | bytes 393224 | tf_op jit(solution)/shard_map/ppermute | solution.py:476
  30.9 0.1 collective-permute-start.12
  31.0 6.7 %collective-permute-done.12 = f32[192,128]{1,0:T(8,128)S(1)} collective-permute-done((f32[192,128]{1,0:T(8,128)S(1)}, f32[192,128]{1,0:T(8,128)S(1)}, u32[]{:S(2)}, u32[]{:S(2)}) %collective-permute-start.12) | collective-permute-done | bytes 98336 | tf_op jit(solution)/shard_map/ppermute | solution.py:476
  37.7 5.9 %collective-permute-start.13 = (f32[192,128]{1,0:T(8,128)S(1)}, f32[192,128]{1,0:T(8,128)S(1)}, u32[]{:S(2)}, u32[]{:S(2)}) collective-permute-start(f32[192,128]{1,0:T(8,128)S(1)} %add.57), channel_id=1, source_target_pairs={{0,8},{1,9},{2,10},{3,11},{4,6},{5,7},{6,4},{7,5},{8,0},{9,1},{10,... | collective-permute-start | bytes 294920 | tf_op jit(solution)/shard_map/ppermute | solution.py:476
  43.6 0.1 collective-permute-start.8
  43.7 2.5 %collective-permute-done.13 = f32[192,128]{1,0:T(8,128)S(1)} collective-permute-done((f32[192,128]{1,0:T(8,128)S(1)}, f32[192,128]{1,0:T(8,128)S(1)}, u32[]{:S(2)}, u32[]{:S(2)}) %collective-permute-start.13) | collective-permute-done | bytes 98336 | tf_op jit(solution)/shard_map/ppermute | solution.py:476
  46.2 0.6 collective-permute-start.14
  46.7 1.9 %collective-permute-done.8 = f32[256,128]{1,0:T(8,128)S(1)} collective-permute-done((f32[256,128]{1,0:T(8,128)S(1)}, f32[256,128]{1,0:T(8,128)S(1)}, u32[]{:S(2)}, u32[]{:S(2)}) %collective-permute-start.8) | collective-permute-done | bytes 131104 | tf_op jit(solution)/shard_map/ppermute | solution.py:476
  48.6 0.6 collective-permute-start.9
  49.2 1.6 %collective-permute-done.14 = f32[192,128]{1,0:T(8,128)S(1)} collective-permute-done((f32[192,128]{1,0:T(8,128)S(1)}, f32[192,128]{1,0:T(8,128)S(1)}, u32[]{:S(2)}, u32[]{:S(2)}) %collective-permute-start.14) | collective-permute-done | bytes 98336 | tf_op jit(solution)/shard_map/ppermute | solution.py:476
  50.9 0.1 collective-permute-start.15
  50.9 2.7 %collective-permute-done.9 = f32[256,128]{1,0:T(8,128)S(1)} collective-permute-done((f32[256,128]{1,0:T(8,128)S(1)}, f32[256,128]{1,0:T(8,128)S(1)}, u32[]{:S(2)}, u32[]{:S(2)}) %collective-permute-start.9) | collective-permute-done | bytes 131104 | tf_op jit(solution)/shard_map/ppermute | solution.py:476
  53.8 1.8 %collective-permute-done.15 = f32[192,128]{1,0:T(8,128)S(1)} collective-permute-done((f32[192,128]{1,0:T(8,128)S(1)}, f32[192,128]{1,0:T(8,128)S(1)}, u32[]{:S(2)}, u32[]{:S(2)}) %collective-permute-start.15) | collective-permute-done | bytes 98336 | tf_op jit(solution)/shard_map/ppermute | solution.py:476
  55.6 1.3 %collective-permute-done.16.refs_2_ = f32[192,128]{1,0:T(8,128)S(1)} collective-permute-done((f32[192,128]{1,0:T(8,128)S(1)}, f32[192,128]{1,0:T(8,128)S(1)}, u32[]{:S(2)}, u32[]{:S(2)}) %collective-permute-start.16) | collective-permute-done | bytes 98336 | tf_op jit(solution)/shard_map/ppermute | solution.py:476
  56.9 2.7 %shard_map.59 = (f32[64,256]{1,0:T(8,128)S(1)}, f32[192,256]{1,0:T(8,128)S(1)}) custom-call(s32[4]{0:T(128)S(1)} %pad_add_fusion.flag_ref.refs_0_, f32[192,128]{1,0:T(8,128)S(1)} %add.60.refs_1_, f32[192,128]{1,0:T(8,128)S(1)} %collective-permute-done.16.refs_2_), custom_call_target="tpu_custom_call" | custom-call | tf_op jit(solution)/shard_map/pallas_call | solution.py:389
  59.6 2.1 %shard_map.60 = (f32[64,256]{1,0:T(8,128)S(1)}, f32[128,256]{1,0:T(8,128)S(1)}) custom-call(f32[192,256]{1,0:T(8,128)S(1)} %get-tuple-element.39.refs_0_), custom_call_target="tpu_custom_call" | custom-call | tf_op jit(solution)/shard_map/pallas_call | solution.py:389
  61.7 2.1 %shard_map.61 = (f32[64,256]{1,0:T(8,128)S(1)}, f32[64,256]{1,0:T(8,128)S(1)}) custom-call(f32[128,256]{1,0:T(8,128)S(1)} %get-tuple-element.41.refs_0_), custom_call_target="tpu_custom_call" | custom-call | tf_op jit(solution)/shard_map/pallas_call | solution.py:389
  63.9 1.8 %shard_map.62.refs_3_ = f32[64,256]{1,0:T(8,128)S(1)} custom-call(f32[64,256]{1,0:T(8,128)S(1)} %get-tuple-element.43.refs_0_), custom_call_target="tpu_custom_call" | custom-call | tf_op jit(solution)/shard_map/pallas_call | solution.py:389
  65.7 2.8 %finish.1 = (bf16[2048,256]{1,0:T(8,128)(2,1)}, f32[256,256]{1,0:T(8,128)}) custom-call(s32[4]{0:T(128)S(1)} %pad_add_fusion.flag_ref.refs_0_, f32[256,128]{1,0:T(8,128)S(1)} %add.55.part_ref, f32[256,128]{1,0:T(8,128)S(1)} %collective-permute-done.10.other_ref, bf16[1024,512]{1,0:T(8,128)(2,1)S(1)} %get-tuple-element.34.image0_ref, ...), custom_call_target="tpu_custom_call" | custom-call | tf_op jit(solution)/shard_map/finish/pallas_call | solution.py:450
  (22 shorter events, 0.3 us)
Async XLA Ops:
  4.9 8.1 %collective-permute-start = (bf16[16,16,256]{2,1,0:T(8,128)(2,1)S(1)}, bf16[16,16,256]{2,1,0:T(8,128)(2,1)S(1)}, u32[]{:S(2)}, u32[]{:S(2)}) collective-permute-start(bf16[16,16,256]{2,1,0:T(8,128)(2,1)S(1)} %get-tuple-element.25), channel_id=1, source_target_pairs={{0,16},{16,0},{1,17},{17,1},{2,18},{18,2},{3,19},{19,3},{4,20},{20... | collective-permute-start | bytes 393224 | tf_op jit(solution)/shard_map/ppermute | solution.py:515
  8.0 3.0 %collective-permute-start.1 = (bf16[8,16,256]{2,1,0:T(8,128)(2,1)S(1)}, bf16[8,16,256]{2,1,0:T(8,128)(2,1)S(1)}, u32[]{:S(2)}, u32[]{:S(2)}) collective-permute-start(bf16[8,16,256]{2,1,0:T(8,128)(2,1)S(1)} %get-tuple-element.26), channel_id=1, source_target_pairs={{0,4},{4,0},{8,12},{12,8},{1,5},{5,1},{9,13},{13,9},{2,6},{6,2},{1... | collective-permute-start | bytes 196616 | tf_op jit(solution)/shard_map/ppermute | solution.py:515
  8.0 3.0 %collective-permute-start.2 = (bf16[8,16,256]{2,1,0:T(8,128)(2,1)S(1)}, bf16[8,16,256]{2,1,0:T(8,128)(2,1)S(1)}, u32[]{:S(2)}, u32[]{:S(2)}) collective-permute-start(bf16[8,16,256]{2,1,0:T(8,128)(2,1)S(1)} %get-tuple-element.27), channel_id=1, source_target_pairs={{4,8},{8,4},{5,9},{9,5},{6,10},{10,6},{7,11},{11,7},{20,24},{24,20... | collective-permute-start | bytes 196616 | tf_op jit(solution)/shard_map/ppermute | solution.py:515
  8.6 4.3 %collective-permute-start.3 = (bf16[8,16,256]{2,1,0:T(8,128)(2,1)S(1)}, bf16[8,16,256]{2,1,0:T(8,128)(2,1)S(1)}, u32[]{:S(2)}, u32[]{:S(2)}) collective-permute-start(bf16[8,16,256]{2,1,0:T(8,128)(2,1)S(1)} %get-tuple-element.28), channel_id=1, source_target_pairs={{0,1},{1,0},{2,3},{3,2},{4,5},{5,4},{6,7},{7,6},{8,9},{9,8},{10,11... | collective-permute-start | bytes 196616 | tf_op jit(solution)/shard_map/ppermute | solution.py:515
  10.3 2.7 %collective-permute-start.4 = (bf16[8,16,256]{2,1,0:T(8,128)(2,1)S(1)}, bf16[8,16,256]{2,1,0:T(8,128)(2,1)S(1)}, u32[]{:S(2)}, u32[]{:S(2)}) collective-permute-start(bf16[8,16,256]{2,1,0:T(8,128)(2,1)S(1)} %get-tuple-element.29), channel_id=1, source_target_pairs={{1,2},{2,1},{5,6},{6,5},{9,10},{10,9},{13,14},{14,13},{17,18},{18,... | collective-permute-start | bytes 196616 | tf_op jit(solution)/shard_map/ppermute | solution.py:515
  17.2 2.8 %collective-permute-start.5 = (f32[256,128]{1,0:T(8,128)S(1)}, f32[256,128]{1,0:T(8,128)S(1)}, u32[]{:S(2)}, u32[]{:S(2)}) collective-permute-start(f32[256,128]{1,0:T(8,128)S(1)} %get-tuple-element.33), channel_id=1, source_target_pairs={{0,4},{1,5},{2,6},{3,7},{4,0},{5,1},{6,2},{7,3},{8,12},{9,13},{10,... | collective-permute-start | bytes 393224 | tf_op jit(solution)/shard_map/ppermute | solution.py:476
  20.0 7.6 %collective-permute-start.6 = (f32[256,128]{1,0:T(8,128)S(1)}, f32[256,128]{1,0:T(8,128)S(1)}, u32[]{:S(2)}, u32[]{:S(2)}) collective-permute-start(f32[256,128]{1,0:T(8,128)S(1)} %add.51), channel_id=1, source_target_pairs={{0,1},{1,0},{2,3},{3,2},{4,20},{5,21},{6,22},{7,23},{8,9},{9,8},{1... | collective-permute-start | bytes 393224 | tf_op jit(solution)/shard_map/ppermute | solution.py:476
  24.6 6.2 %collective-permute-start.11 = (f32[192,128]{1,0:T(8,128)S(1)}, f32[192,128]{1,0:T(8,128)S(1)}, u32[]{:S(2)}, u32[]{:S(2)}) collective-permute-start(f32[192,128]{1,0:T(8,128)S(1)} %get-tuple-element.37), channel_id=1, source_target_pairs={{0,4},{1,5},{2,6},{3,7},{4,0},{5,1},{6,2},{7,3},{8,12},{9,13},{10,... | collective-permute-start | bytes 294920 | tf_op jit(solution)/shard_map/ppermute | solution.py:476
  27.6 15.9 %collective-permute-start.7 = (f32[256,128]{1,0:T(8,128)S(1)}, f32[256,128]{1,0:T(8,128)S(1)}, u32[]{:S(2)}, u32[]{:S(2)}) collective-permute-start(f32[256,128]{1,0:T(8,128)S(1)} %add.52), channel_id=1, source_target_pairs={{0,2},{1,3},{2,0},{3,1},{4,12},{5,13},{6,14},{7,15},{8,10},{9,11},... | collective-permute-start | bytes 393224 | tf_op jit(solution)/shard_map/ppermute | solution.py:476
  30.9 6.8 %collective-permute-start.12 = (f32[192,128]{1,0:T(8,128)S(1)}, f32[192,128]{1,0:T(8,128)S(1)}, u32[]{:S(2)}, u32[]{:S(2)}) collective-permute-start(f32[192,128]{1,0:T(8,128)S(1)} %add.56), channel_id=1, source_target_pairs={{0,2},{1,3},{2,0},{3,1},{4,12},{5,13},{6,14},{7,15},{8,10},{9,11},... | collective-permute-start | bytes 294920 | tf_op jit(solution)/shard_map/ppermute | solution.py:476
  37.7 8.5 %collective-permute-start.13 = (f32[192,128]{1,0:T(8,128)S(1)}, f32[192,128]{1,0:T(8,128)S(1)}, u32[]{:S(2)}, u32[]{:S(2)}) collective-permute-start(f32[192,128]{1,0:T(8,128)S(1)} %add.57), channel_id=1, source_target_pairs={{0,8},{1,9},{2,10},{3,11},{4,6},{5,7},{6,4},{7,5},{8,0},{9,1},{10,... | collective-permute-start | bytes 294920 | tf_op jit(solution)/shard_map/ppermute | solution.py:476
  43.6 5.0 %collective-permute-start.8 = (f32[256,128]{1,0:T(8,128)S(1)}, f32[256,128]{1,0:T(8,128)S(1)}, u32[]{:S(2)}, u32[]{:S(2)}) collective-permute-start(f32[256,128]{1,0:T(8,128)S(1)} %add.53), channel_id=1, source_target_pairs={{0,8},{1,9},{2,10},{3,11},{4,6},{5,7},{6,4},{7,5},{8,0},{9,1},{10,... | collective-permute-start | bytes 393224 | tf_op jit(solution)/shard_map/ppermute | solution.py:476
  46.2 4.7 %collective-permute-start.14 = (f32[192,128]{1,0:T(8,128)S(1)}, f32[192,128]{1,0:T(8,128)S(1)}, u32[]{:S(2)}, u32[]{:S(2)}) collective-permute-start(f32[192,128]{1,0:T(8,128)S(1)} %add.58), channel_id=1, source_target_pairs={{0,16},{1,17},{2,18},{3,19},{4,5},{5,4},{6,7},{7,6},{8,24},{9,25},... | collective-permute-start | bytes 294920 | tf_op jit(solution)/shard_map/ppermute | solution.py:476
  48.6 5.0 %collective-permute-start.9 = (f32[256,128]{1,0:T(8,128)S(1)}, f32[256,128]{1,0:T(8,128)S(1)}, u32[]{:S(2)}, u32[]{:S(2)}) collective-permute-start(f32[256,128]{1,0:T(8,128)S(1)} %add.54), channel_id=1, source_target_pairs={{0,16},{1,17},{2,18},{3,19},{4,5},{5,4},{6,7},{7,6},{8,24},{9,25},... | collective-permute-start | bytes 393224 | tf_op jit(solution)/shard_map/ppermute | solution.py:476
  50.9 4.7 %collective-permute-start.15 = (f32[192,128]{1,0:T(8,128)S(1)}, f32[192,128]{1,0:T(8,128)S(1)}, u32[]{:S(2)}, u32[]{:S(2)}) collective-permute-start(f32[192,128]{1,0:T(8,128)S(1)} %add.59), channel_id=1, source_target_pairs={{0,1},{1,0},{2,3},{3,2},{4,20},{5,21},{6,22},{7,23},{8,9},{9,8},{1... | collective-permute-start | bytes 294920 | tf_op jit(solution)/shard_map/ppermute | solution.py:476
  53.7 12.0 %collective-permute-start.10 = (f32[256,128]{1,0:T(8,128)S(1)}, f32[256,128]{1,0:T(8,128)S(1)}, u32[]{:S(2)}, u32[]{:S(2)}) collective-permute-start(f32[256,128]{1,0:T(8,128)S(1)} %add.55.part_ref), channel_id=1, source_target_pairs={{0,4},{1,5},{2,6},{3,7},{4,0},{5,1},{6,2},{7,3},{8,12},{9,13},{10,... | collective-permute-start | bytes 393224 | tf_op jit(solution)/shard_map/ppermute | solution.py:476
  55.6 1.4 %collective-permute-start.16 = (f32[192,128]{1,0:T(8,128)S(1)}, f32[192,128]{1,0:T(8,128)S(1)}, u32[]{:S(2)}, u32[]{:S(2)}) collective-permute-start(f32[192,128]{1,0:T(8,128)S(1)} %add.60.refs_1_), channel_id=1, source_target_pairs={{0,4},{1,5},{2,6},{3,7},{4,0},{5,1},{6,2},{7,3},{8,12},{9,13},{10,... | collective-permute-start | bytes 294920 | tf_op jit(solution)/shard_map/ppermute | solution.py:476
